TPU v7x, 128 devices: a whole 4x4x4 slice. The times are simulated.
128 devices in a mesh: gx: 8 (over z, x_lo), gy: 4 (over x_hi, core), ha: 4 (over y).
Axes of the slice: x: 4 (x_hi: 2, x_lo: 2; x = x_hi * 2 + x_lo), y: 4, z: 4, core: 2. Of those that a mesh axis runs over, the one named last changes fastest.
Arguments:
- tokens: bfloat16 [64, 64, 16, 384], P('gx', 'gy'), may hold values from -30 to 30
- input_weight: bfloat16 [384, 768], P(None, 'ha'), may hold values from -1 to 1
- output_weight: bfloat16 [256, 384], P('ha'), may hold values from -0.375 to 0.375
- tissue_bits: int32 [64, 64], P('gx', 'gy'), may hold values from 0 to 65535
- cotangent: bfloat16 [64, 64, 16, 384], P('gx', 'gy'), may hold values from -6 to 6
Outputs:
- token_gradient: bfloat16 [64, 64, 16, 384], P('gx', 'gy', None, 'ha')
- input_gradient: float32 [384, 768], P(None, 'ha')
- output_gradient: float32 [256, 384], P('ha')
All inputs are finite; a program needn't handle non-finite values.
Results may differ from a plain program's by a relative error of at most 0.018.
The roundings to bfloat16 on the way count: a program that leaves them out, or rounds other values in their place, can miss the bound.
Values may be sent and summed in bfloat16 or wider, within the bound.
No kernel may reach another device: no remote copies, remote signals or barrier semaphores. Data moves between devices by JAX's collectives and lax.ppermute only.
A program may use at most 128 MiB of HBM per device.

v0:
```python
import jax
import jax.numpy as jnp
from jax import lax
from jax.sharding import PartitionSpec as P

HD = 64
REACH = 3


def extended(block, sides, width):
    for axis, dim in sides:
        count = lax.axis_size(axis)
        forward = [(i, i + 1) for i in range(count - 1)]
        backward = [(target, source) for source, target in forward]
        low = lax.ppermute(
            lax.slice_in_dim(block, block.shape[dim] - width, None, axis=dim), axis, forward
        )
        high = lax.ppermute(lax.slice_in_dim(block, 0, width, axis=dim), axis, backward)
        block = jnp.concatenate([low, block, high], axis=dim)
    return block


def block_length(extent, plane_rows):
    for length in range(1, extent + 1):
        if extent % length == 0 and length * plane_rows >= 512:
            return length
    return extent


def shards(tokens, input_weight, output_weight, tissue_bits, cotangent):
    width_x, width_y, depth, model_width = tokens.shape
    local_heads = output_weight.shape[0] // HD
    token_count = width_x * width_y * depth
    score_scale = HD ** (-0.5)
    flat_tokens = tokens.reshape(token_count, model_width)
    flat_cotangent = cotangent.reshape(token_count, model_width)
    bit_values = 2 ** jnp.arange(depth, dtype=jnp.int32)
    key_valid = (tissue_bits[:, :, None] // bit_values % 2).astype(jnp.bfloat16)
    key_span_x_full = width_x + 2 * REACH
    key_span_y = width_y + 2 * REACH
    projected = jnp.dot(flat_tokens, input_weight, preferred_element_type=jnp.float32).astype(
        jnp.bfloat16
    )
    projected = projected.reshape(token_count, local_heads, 3, HD)
    queries = projected[:, :, 0, :].reshape(token_count, local_heads * HD)
    pair_local = projected[:, :, 1:, :].reshape(width_x, width_y, depth, local_heads * 2 * HD)
    pair_padded, valid_padded = (
        extended(pair_local, (("gx", 0), ("gy", 1)), REACH),
        extended(key_valid, (("gx", 0), ("gy", 1)), REACH),
    )
    upstream = jnp.einsum(
        "nd,ed->ne", flat_cotangent, output_weight, preferred_element_type=jnp.float32
    ).astype(jnp.bfloat16)
    block_x = block_length(width_x, width_y * depth)
    block_count = width_x // block_x
    key_span_x = block_x + 2 * REACH
    query_rows = block_x * width_y * depth
    key_rows = key_span_x * key_span_y * depth
    query_slots = jnp.arange(query_rows)
    query_x = query_slots // (width_y * depth)
    query_y = query_slots // depth % width_y
    query_z = query_slots % depth
    key_slots = jnp.arange(key_rows)
    key_x = key_slots // (key_span_y * depth) - REACH
    key_y = key_slots // depth % key_span_y - REACH
    key_z = key_slots % depth
    within = (
        (jnp.abs(query_x[:, None] - key_x[None, :]) <= REACH)
        & (jnp.abs(query_y[:, None] - key_y[None, :]) <= REACH)
        & (jnp.abs(query_z[:, None] - key_z[None, :]) <= REACH)
    )
    self_pair = (
        (query_x[:, None] == key_x[None, :])
        & (query_y[:, None] == key_y[None, :])
        & (query_z[:, None] == key_z[None, :])
    )
    query_grid = queries.reshape(width_x, width_y, depth, local_heads, HD)
    upstream_grid = upstream.reshape(width_x, width_y, depth, local_heads, HD)
    pair_grid = pair_padded.reshape(key_span_x_full, key_span_y, depth, local_heads, 2, HD)

    def attend_block(block_index, carry):
        query_sums, pair_sums, outputs = carry
        first_row = block_index * block_x
        query_block = lax.dynamic_slice_in_dim(query_grid, first_row, block_x, 0).reshape(
            query_rows, local_heads, HD
        )
        upstream_block = lax.dynamic_slice_in_dim(upstream_grid, first_row, block_x, 0).reshape(
            query_rows, local_heads, HD
        )
        pair_block = lax.dynamic_slice_in_dim(pair_grid, first_row, key_span_x, 0).reshape(
            key_rows, local_heads, 2, HD
        )
        keys_block = pair_block[:, :, 0, :]
        values_block = pair_block[:, :, 1, :]
        live_keys = (
            lax.dynamic_slice_in_dim(valid_padded, first_row, key_span_x, 0).reshape(key_rows) > 0
        )
        allowed = within & (live_keys[None, :] | self_pair)
        scores = (
            jnp.einsum("qhe,khe->hqk", query_block, keys_block, preferred_element_type=jnp.float32)
            * score_scale
        )
        scores = jnp.where(allowed[None], scores, -jnp.inf)
        row_max = jnp.max(scores, axis=-1, keepdims=True)
        raised = jnp.exp(scores - row_max)
        weights = (raised / jnp.sum(raised, axis=-1, keepdims=True)).astype(jnp.bfloat16)
        result = jnp.einsum(
            "hqk,khe->qhe", weights, values_block, preferred_element_type=jnp.float32
        )
        weight_gradient = jnp.einsum(
            "qhe,khe->hqk", upstream_block, values_block, preferred_element_type=jnp.float32
        )
        row_inner = jnp.sum(upstream_block.astype(jnp.float32) * result, axis=-1)
        score_gradient = (
            weights.astype(jnp.float32) * (weight_gradient - row_inner.T[:, :, None]) * score_scale
        ).astype(jnp.bfloat16)
        query_gradient = jnp.einsum(
            "hqk,khe->qhe", score_gradient, keys_block, preferred_element_type=jnp.float32
        )
        key_gradient = jnp.einsum(
            "hqk,qhe->khe", score_gradient, query_block, preferred_element_type=jnp.float32
        )
        value_gradient = jnp.einsum(
            "hqk,qhe->khe", weights, upstream_block, preferred_element_type=jnp.float32
        )
        pair_gradient = jnp.stack([key_gradient, value_gradient], axis=2).reshape(
            key_span_x, key_span_y, depth, local_heads * 2 * HD
        )
        query_sums = lax.dynamic_update_slice_in_dim(
            query_sums,
            query_gradient.reshape(block_x, width_y, depth, local_heads * HD),
            first_row,
            0,
        )
        previous = lax.dynamic_slice_in_dim(pair_sums, first_row, key_span_x, 0)
        pair_sums = lax.dynamic_update_slice_in_dim(
            pair_sums, previous + pair_gradient, first_row, 0
        )
        outputs = lax.dynamic_update_slice_in_dim(
            outputs,
            result.astype(jnp.bfloat16).reshape(block_x, width_y, depth, local_heads * HD),
            first_row,
            0,
        )
        return (query_sums, pair_sums, outputs)

    start = (
        jnp.zeros((width_x, width_y, depth, local_heads * HD), jnp.float32),
        jnp.zeros((key_span_x_full, key_span_y, depth, local_heads * 2 * HD), jnp.float32),
        jnp.zeros((width_x, width_y, depth, local_heads * HD), jnp.bfloat16),
    )
    query_sums, pair_sums, outputs = lax.fori_loop(0, block_count, attend_block, start)
    rims_first = jnp.concatenate([pair_sums[:REACH], pair_sums[width_x + REACH :]], axis=0)
    from_first = extended(rims_first.astype(jnp.bfloat16), (("gx", 0),), REACH).astype(
        rims_first.dtype
    )
    interior = pair_sums[REACH : width_x + REACH]
    interior = interior.at[:REACH].add(from_first[:REACH])
    interior = interior.at[width_x - REACH :].add(from_first[3 * REACH :])
    rims_second = jnp.concatenate([interior[:, :REACH], interior[:, width_y + REACH :]], axis=1)
    from_second = extended(rims_second.astype(jnp.bfloat16), (("gy", 1),), REACH).astype(
        rims_second.dtype
    )
    centre = interior[:, REACH : width_y + REACH]
    centre = centre.at[:, :REACH].add(from_second[:, :REACH])
    centre = centre.at[:, width_y - REACH :].add(from_second[:, 3 * REACH :])
    query_part = query_sums.reshape(token_count, local_heads, 1, HD)
    pair_part = centre.reshape(token_count, local_heads, 2, HD)
    dprojected = (
        jnp.concatenate([query_part, pair_part], axis=2)
        .reshape(token_count, local_heads * 3 * HD)
        .astype(jnp.bfloat16)
    )
    partial_terms = jnp.einsum(
        "nc,dc->nd", dprojected, input_weight, preferred_element_type=jnp.float32
    ).reshape(width_x, width_y, depth, model_width)
    token_gradient = lax.psum_scatter(partial_terms, "ha", scatter_dimension=3, tiled=True).astype(
        jnp.bfloat16
    )
    attended_flat = outputs.reshape(token_count, local_heads * HD)
    part_input = jnp.einsum(
        "nd,nc->dc", flat_tokens, dprojected, preferred_element_type=jnp.float32
    )
    part_output = jnp.einsum(
        "ne,nd->ed", attended_flat, flat_cotangent, preferred_element_type=jnp.float32
    )
    summed_input, summed_output = (
        lax.psum(part_input.astype(jnp.bfloat16), ("gx", "gy")).astype(jnp.float32),
        lax.psum(part_output.astype(jnp.bfloat16), ("gx", "gy")).astype(jnp.float32),
    )
    normaliser = (token_count * lax.axis_size("gx") * lax.axis_size("gy")) ** (-0.5)
    return (token_gradient, summed_input * normaliser, summed_output * normaliser)


def solution(mesh):
    placed = (
        P("gx", "gy", None, None),
        P(None, "ha"),
        P("ha", None),
        P("gx", "gy"),
        P("gx", "gy", None, None),
    )
    return jax.shard_map(
        shards,
        mesh=mesh,
        in_specs=placed,
        out_specs=(P("gx", "gy", None, "ha"), P(None, "ha"), P("ha", None)),
        check_vma=False,
    )
```

profile of v0, /device:TPU:0, one launch (start us, length us, event | category | flops | bytes accessed | tf_op | source)
XLA Modules:
  0.0 429.6 jit_solution(15858001204018962524)
XLA Ops:
  8.9 1.5 fusion.17
  11.0 3.5 collective-permute-start.4
  14.5 1.3 collective-permute-start.5
  15.8 1.7 convolution_convert_fusion
  24.8 5.9 %collective-permute-start = (bf16[3,16,16,128]{3,2,1,0:T(8,128)(2,1)}, bf16[3,16,16,128]{3,2,1,0:T(8,128)(2,1)}, u32[]{:S(2)}, u32[]{:S(2)}) collective-permute-start(bf16[3,16,16,128]{3,2,1,0:T(8,128)(2,1)} %slice.209), channel_id=1, source_target_pairs={{0,16},{16,32},{32,48},{48,64},{64,80},{80,96},{96,112},{1,17},{17... | collective-permute-start | bytes 589832 | tf_op jit(solution)/shard_map/ppermute | solution.py:15
  31.3 1.4 convolution_convert_fusion.1
  41.4 6.2 %collective-permute-start.2 = (bf16[14,3,16,128]{3,2,1,0:T(8,128)(2,1)S(1)}, bf16[14,3,16,128]{3,2,1,0:T(8,128)(2,1)S(1)}, u32[]{:S(2)}, u32[]{:S(2)}) collective-permute-start(bf16[14,3,16,128]{3,2,1,0:T(8,128)(2,1)S(1)} %get-tuple-element.401), channel_id=1, source_target_pairs={{0,4},{4,8},{8,12},{1,5},{5,9},{9,13},{2,6},{6,10},{10,14},{3,7},{... | collective-permute-start | bytes 516104 | tf_op jit(solution)/shard_map/ppermute | solution.py:15
  52.0 1.4 pad_maximum_fusion.8
  53.7 1.4 pad_maximum_fusion.1
  55.1 2.1 reshape.485
  59.0 1.7 broadcast_in_dim.27
  60.7 128.2 %while.23 = (s32[]{:T(128)}, bf16[8,16,16,64]{3,2,1,0:T(8,128)(2,1)}, f32[14,22,16,128]{3,2,1,0:T(8,128)}, bf16[8,16,16,64]{3,2,1,0:T(8,128)(2,1)}, bf16[14,22,1...) while((s32[]{:T(128)}, ...), condition=%wide.region_4.5_spmd.clone.clone, body=%wide.region_0.4_spmd.clone.clone.sunk | while | flops 1152845056 | bytes 82846784 | solution.py:152
  63.6 2.5 constant_dynamic-slice_fusion.8
  66.3 5.8 %fusion.85 = (f32[512]{0:T(512)S(1)}, f32[512,2816]{1,0:T(8,128)S(1)}) fusion(bf16[512,64]{1,0:T(8,128)(2,1)S(1)} %bitcast.150, bf16[2816,1,2,64]{3,0,2,1:T(8,128)(2,1)S(1)} %bitcast.143, pred[2816]{0:T(1024)(128)(4,1)S(1)} %gt.22, s32[2816]{0:T(1024)S(1)} %get-tuple-element.564, s32[512]{0:T(512)S(1)} %get-tuple-element.565, ...), kind=kOutput, calls=%fused_computation.123.clone.1 | convolution fusion | flops 214826496 | bytes 6667264 | tf_op jit(solution)/shard_map/while/body/eval_jaxpr/qhe,khe->hqk/dot_general | solution.py:100
  73.0 1.5 divide_convert_fusion.2
  74.5 1.5 copy-done.1
  77.2 2.6 convolution_bitcast_fusion.9
  83.6 3.3 copy.74
  86.9 3.2 reshape.514
  90.1 2.7 add_dynamic-update-slice_fusion.2
  95.7 2.5 constant_dynamic-slice_fusion.8
  98.4 5.8 %fusion.85 = (f32[512]{0:T(512)S(1)}, f32[512,2816]{1,0:T(8,128)S(1)}) fusion(bf16[512,64]{1,0:T(8,128)(2,1)S(1)} %bitcast.150, bf16[2816,1,2,64]{3,0,2,1:T(8,128)(2,1)S(1)} %bitcast.143, pred[2816]{0:T(1024)(128)(4,1)S(1)} %gt.22, s32[2816]{0:T(1024)S(1)} %get-tuple-element.564, s32[512]{0:T(512)S(1)} %get-tuple-element.565, ...), kind=kOutput, calls=%fused_computation.123.clone.1 | convolution fusion | flops 214826496 | bytes 6667264 | tf_op jit(solution)/shard_map/while/body/eval_jaxpr/qhe,khe->hqk/dot_general | solution.py:100
  105.1 1.5 divide_convert_fusion.2
  106.6 1.5 copy-done.1
  109.3 2.6 convolution_bitcast_fusion.9
  115.7 3.3 copy.74
  119.0 3.2 reshape.514
  122.2 2.7 add_dynamic-update-slice_fusion.2
  127.8 2.5 constant_dynamic-slice_fusion.8
  130.4 5.8 %fusion.85 = (f32[512]{0:T(512)S(1)}, f32[512,2816]{1,0:T(8,128)S(1)}) fusion(bf16[512,64]{1,0:T(8,128)(2,1)S(1)} %bitcast.150, bf16[2816,1,2,64]{3,0,2,1:T(8,128)(2,1)S(1)} %bitcast.143, pred[2816]{0:T(1024)(128)(4,1)S(1)} %gt.22, s32[2816]{0:T(1024)S(1)} %get-tuple-element.564, s32[512]{0:T(512)S(1)} %get-tuple-element.565, ...), kind=kOutput, calls=%fused_computation.123.clone.1 | convolution fusion | flops 214826496 | bytes 6667264 | tf_op jit(solution)/shard_map/while/body/eval_jaxpr/qhe,khe->hqk/dot_general | solution.py:100
  137.2 1.5 divide_convert_fusion.2
  138.7 1.5 copy-done.1
  141.4 2.6 convolution_bitcast_fusion.9
  147.8 3.3 copy.74
  151.0 3.2 reshape.514
  154.2 2.7 add_dynamic-update-slice_fusion.2
  159.8 2.5 constant_dynamic-slice_fusion.8
  162.5 5.8 %fusion.85 = (f32[512]{0:T(512)S(1)}, f32[512,2816]{1,0:T(8,128)S(1)}) fusion(bf16[512,64]{1,0:T(8,128)(2,1)S(1)} %bitcast.150, bf16[2816,1,2,64]{3,0,2,1:T(8,128)(2,1)S(1)} %bitcast.143, pred[2816]{0:T(1024)(128)(4,1)S(1)} %gt.22, s32[2816]{0:T(1024)S(1)} %get-tuple-element.564, s32[512]{0:T(512)S(1)} %get-tuple-element.565, ...), kind=kOutput, calls=%fused_computation.123.clone.1 | convolution fusion | flops 214826496 | bytes 6667264 | tf_op jit(solution)/shard_map/while/body/eval_jaxpr/qhe,khe->hqk/dot_general | solution.py:100
  169.2 1.5 divide_convert_fusion.2
  170.7 1.5 copy-done.1
  173.4 2.6 convolution_bitcast_fusion.9
  179.8 3.3 copy.74
  183.1 3.2 reshape.514
  186.3 2.7 add_dynamic-update-slice_fusion.2
  188.9 2.0 convert.13
  191.0 3.6 collective-permute-start.8
  196.0 2.5 collective-permute-done.8
  198.5 7.3 %collective-permute-done.9 = bf16[3,22,16,128]{3,2,1,0:T(8,128)(2,1)S(1)} collective-permute-done((bf16[3,22,16,128]{3,2,1,0:T(8,128)(2,1)S(1)}, bf16[3,22,16,128]{3,2,1,0:T(8,128)(2,1)S(1)}, u32[]{:S(2)}, u32[]{:S(2)}) %collective-permute-start.9) | collective-permute-done | bytes 270368 | tf_op jit(solution)/shard_map/ppermute | solution.py:18
  206.8 6.8 %collective-permute-start.10 = (bf16[8,3,16,128]{3,2,1,0:T(8,128)(2,1)}, bf16[8,3,16,128]{3,2,1,0:T(8,128)(2,1)}, u32[]{:S(2)}, u32[]{:S(2)}) collective-permute-start(bf16[8,3,16,128]{3,2,1,0:T(8,128)(2,1)} %get-tuple-element.405), channel_id=1, source_target_pairs={{0,4},{4,8},{8,12},{1,5},{5,9},{9,13},{2,6},{6,10},{10,14},{3,7},{... | collective-permute-start | bytes 294920 | tf_op jit(solution)/shard_map/ppermute | solution.py:15
  216.9 3.0 collective-permute-done.11
  219.9 1.6 fusion.13
  221.5 1.7 fusion.12
  223.3 2.5 reshape.489
  226.6 2.5 copy.55
  230.4 4.1 convert_element_type.112
  234.5 2.4 fusion.14
  236.9 20.4 %copy.58 = f32[8,16,16,384]{2,1,0,3:T(8,128)} copy(f32[8,16,16,384]{3,2,1,0:T(8,128)} %fusion.14) | data formatting | bytes 6291456
  257.2 21.8 %reshape.511 = f32[384,2048]{1,0:T(8,128)} reshape(f32[384,8,16,16]{3,2,1,0:T(8,128)} %bitcast.147) | data formatting | bytes 6291456
  279.1 1.4 copy-done.5
  280.5 1.4 fusion.9
  281.9 128.5 %psum.15 = bf16[64,384]{1,0:T(8,128)(2,1)S(1)} all-reduce(bf16[64,384]{1,0:T(8,128)(2,1)S(1)} %fusion.9), channel_id=1, replica_groups=mesh['gx'=8,'gy'=4,'ha'=4] {'gx','gy'}, use_global_device_ids=true, to_apply=%region_7.8 | all-reduce | flops 24576 | bytes 98304 | tf_op jit(solution)/shard_map/psum | solution.py:189
  411.1 1.6 convert_multiply_fusion
  412.7 4.7 %reshape.512 = bf16[96,8,16,16]{3,2,1,0:T(8,128)(2,1)} reshape(f32[96,2048]{1,0:T(8,128)} %reduce-scatter.4.cloned.1.call-done) | data formatting | bytes 1179648
  417.4 4.8 %copy.59 = bf16[8,16,16,96]{3,2,1,0:T(8,128)(2,1)} copy(bf16[8,16,16,96]{2,1,0,3:T(8,128)(2,1)} %bitcast.154) | data formatting | bytes 786432
  (157 shorter events, 68.5 us)
Async XLA Ops:
  8.0 7.8 %copy-start = (bf16[8,16,16,384]{3,2,1,0:T(8,128)(2,1)S(1)}, bf16[8,16,16,384]{3,2,1,0:T(8,128)(2,1)}, u32[]{:S(2)}) copy-start(bf16[8,16,16,384]{3,2,1,0:T(8,128)(2,1)} %param.15) | copy-start | bytes 4718596
  8.0 403.1 %all-reduce.2.cloned.1.call-start = ((), (), s32[]{:S(2)}) async-start(), calls=%async_computation.1 | async-start | bytes 294912 | tf_op jit(solution)/shard_map/psum | solution.py:188
  10.3 5.4 %copy-start.11 = (bf16[8,16,16]{2,1,0:T(8,128)(2,1)}, bf16[8,16,16]{2,1,0:T(8,128)(2,1)S(1)}, u32[]{:S(2)}) copy-start(bf16[8,16,16]{2,1,0:T(8,128)(2,1)S(1)} %fusion.17) | copy-start | bytes 12292
  11.0 24.1 %collective-permute-start.4 = (bf16[3,16,16]{2,1,0:T(8,128)(2,1)}, bf16[3,16,16]{2,1,0:T(8,128)(2,1)S(1)}, u32[]{:S(2)}, u32[]{:S(2)}) collective-permute-start(bf16[3,16,16]{2,1,0:T(8,128)(2,1)} %get-tuple-element.409), channel_id=1, source_target_pairs={{0,16},{16,32},{32,48},{48,64},{64,80},{80,96},{96,112},{1,17},{17... | collective-permute-start | bytes 4616 | tf_op jit(solution)/shard_map/ppermute | solution.py:15
  14.5 20.6 %collective-permute-start.5 = (bf16[3,16,16]{2,1,0:T(8,128)(2,1)}, bf16[3,16,16]{2,1,0:T(8,128)(2,1)}, u32[]{:S(2)}, u32[]{:S(2)}) collective-permute-start(bf16[3,16,16]{2,1,0:T(8,128)(2,1)} %get-tuple-element.410), channel_id=1, source_target_pairs={{16,0},{32,16},{48,32},{64,48},{80,64},{96,80},{112,96},{17,1},{33... | collective-permute-start | bytes 4616 | tf_op jit(solution)/shard_map/ppermute | solution.py:18
  15.8 15.5 %copy-start.4 = (bf16[8,16,16,384]{3,2,1,0:T(8,128)(2,1)S(1)}, bf16[8,16,16,384]{3,2,1,0:T(8,128)(2,1)}, u32[]{:S(2)}) copy-start(bf16[8,16,16,384]{3,2,1,0:T(8,128)(2,1)} %param.19) | copy-start | bytes 4718596
  17.5 0.9 copy-start.6
  21.4 18.1 %collective-permute-start.1 = (bf16[3,16,16,128]{3,2,1,0:T(8,128)(2,1)}, bf16[3,16,16,128]{3,2,1,0:T(8,128)(2,1)}, u32[]{:S(2)}, u32[]{:S(2)}) collective-permute-start(bf16[3,16,16,128]{3,2,1,0:T(8,128)(2,1)} %slice.212), channel_id=1, source_target_pairs={{16,0},{32,16},{48,32},{64,48},{80,64},{96,80},{112,96},{17,1},{33... | collective-permute-start | bytes 589832 | tf_op jit(solution)/shard_map/ppermute | solution.py:18
  24.8 13.6 %collective-permute-start = (bf16[3,16,16,128]{3,2,1,0:T(8,128)(2,1)}, bf16[3,16,16,128]{3,2,1,0:T(8,128)(2,1)}, u32[]{:S(2)}, u32[]{:S(2)}) collective-permute-start(bf16[3,16,16,128]{3,2,1,0:T(8,128)(2,1)} %slice.209), channel_id=1, source_target_pairs={{0,16},{16,32},{32,48},{48,64},{64,80},{80,96},{96,112},{1,17},{17... | collective-permute-start | bytes 589832 | tf_op jit(solution)/shard_map/ppermute | solution.py:15
  32.7 2.4 copy-start.12
  35.8 16.2 %collective-permute-start.6 = (bf16[14,3,16]{2,1,0:T(4,128)(2,1)S(1)}, bf16[14,3,16]{2,1,0:T(4,128)(2,1)S(1)}, u32[]{:S(2)}, u32[]{:S(2)}) collective-permute-start(bf16[14,3,16]{2,1,0:T(4,128)(2,1)S(1)} %get-tuple-element.407), channel_id=1, source_target_pairs={{0,4},{4,8},{8,12},{1,5},{5,9},{9,13},{2,6},{6,10},{10,14},{3,7},{... | collective-permute-start | bytes 4040 | tf_op jit(solution)/shard_map/ppermute | solution.py:15
  37.1 14.9 %collective-permute-start.7 = (bf16[14,3,16]{2,1,0:T(4,128)(2,1)S(1)}, bf16[14,3,16]{2,1,0:T(4,128)(2,1)S(1)}, u32[]{:S(2)}, u32[]{:S(2)}) collective-permute-start(bf16[14,3,16]{2,1,0:T(4,128)(2,1)S(1)} %get-tuple-element.408), channel_id=1, source_target_pairs={{4,0},{8,4},{12,8},{5,1},{9,5},{13,9},{6,2},{10,6},{14,10},{7,3},{... | collective-permute-start | bytes 4040 | tf_op jit(solution)/shard_map/ppermute | solution.py:18
  40.4 0.9 copy-start.7
  41.4 12.0 %collective-permute-start.2 = (bf16[14,3,16,128]{3,2,1,0:T(8,128)(2,1)S(1)}, bf16[14,3,16,128]{3,2,1,0:T(8,128)(2,1)S(1)}, u32[]{:S(2)}, u32[]{:S(2)}) collective-permute-start(bf16[14,3,16,128]{3,2,1,0:T(8,128)(2,1)S(1)} %get-tuple-element.401), channel_id=1, source_target_pairs={{0,4},{4,8},{8,12},{1,5},{5,9},{9,13},{2,6},{6,10},{10,14},{3,7},{... | collective-permute-start | bytes 516104 | tf_op jit(solution)/shard_map/ppermute | solution.py:15
  47.5 6.2 %collective-permute-start.3 = (bf16[14,3,16,128]{3,2,1,0:T(8,128)(2,1)S(1)}, bf16[14,3,16,128]{3,2,1,0:T(8,128)(2,1)}, u32[]{:S(2)}, u32[]{:S(2)}) collective-permute-start(bf16[14,3,16,128]{3,2,1,0:T(8,128)(2,1)S(1)} %get-tuple-element.402), channel_id=1, source_target_pairs={{4,0},{8,4},{12,8},{5,1},{9,5},{13,9},{6,2},{10,6},{14,10},{7,3},{... | collective-permute-start | bytes 516104 | tf_op jit(solution)/shard_map/ppermute | solution.py:18
  57.2 3.5 copy-start.13
  74.5 1.5 copy-start.1
  77.2 2.7 copy-start.2
  106.6 1.5 copy-start.1
  109.3 2.7 copy-start.2
  138.7 1.5 copy-start.1
  141.4 2.7 copy-start.2
  170.7 1.5 copy-start.1
  173.4 2.7 copy-start.2
  188.9 7.0 %copy-start.3 = (f32[14,22,16,128]{3,2,1,0:T(8,128)S(1)}, f32[14,22,16,128]{3,2,1,0:T(8,128)}, u32[]{:S(2)}) copy-start(f32[14,22,16,128]{3,2,1,0:T(8,128)} %get-tuple-element.223) | copy-start | bytes 7569412
  191.0 7.5 %collective-permute-start.8 = (bf16[3,22,16,128]{3,2,1,0:T(8,128)(2,1)S(1)}, bf16[3,22,16,128]{3,2,1,0:T(8,128)(2,1)S(1)}, u32[]{:S(2)}, u32[]{:S(2)}) collective-permute-start(bf16[3,22,16,128]{3,2,1,0:T(8,128)(2,1)S(1)} %get-tuple-element.399), channel_id=1, source_target_pairs={{0,16},{16,32},{32,48},{48,64},{64,80},{80,96},{96,112},{1,17},{17... | collective-permute-start | bytes 811016 | tf_op jit(solution)/shard_map/ppermute | solution.py:15
  194.6 11.3 %collective-permute-start.9 = (bf16[3,22,16,128]{3,2,1,0:T(8,128)(2,1)S(1)}, bf16[3,22,16,128]{3,2,1,0:T(8,128)(2,1)S(1)}, u32[]{:S(2)}, u32[]{:S(2)}) collective-permute-start(bf16[3,22,16,128]{3,2,1,0:T(8,128)(2,1)S(1)} %get-tuple-element.400), channel_id=1, source_target_pairs={{16,0},{32,16},{48,32},{64,48},{80,64},{96,80},{112,96},{17,1},{33... | collective-permute-start | bytes 811016 | tf_op jit(solution)/shard_map/ppermute | solution.py:18
  205.9 9.0 %copy-start.8 = (bf16[8,16,16,64]{3,2,1,0:T(8,128)(2,1)S(1)}, bf16[8,16,16,64]{3,2,1,0:T(8,128)(2,1)}, u32[]{:S(2)}) copy-start(bf16[8,16,16,64]{3,2,1,0:T(8,128)(2,1)} %get-tuple-element.222) | copy-start | bytes 786436
  206.8 10.1 %collective-permute-start.10 = (bf16[8,3,16,128]{3,2,1,0:T(8,128)(2,1)}, bf16[8,3,16,128]{3,2,1,0:T(8,128)(2,1)}, u32[]{:S(2)}, u32[]{:S(2)}) collective-permute-start(bf16[8,3,16,128]{3,2,1,0:T(8,128)(2,1)} %get-tuple-element.405), channel_id=1, source_target_pairs={{0,4},{4,8},{8,12},{1,5},{5,9},{9,13},{2,6},{6,10},{10,14},{3,7},{... | collective-permute-start | bytes 294920 | tf_op jit(solution)/shard_map/ppermute | solution.py:15
  213.6 6.3 %collective-permute-start.11 = (bf16[8,3,16,128]{3,2,1,0:T(8,128)(2,1)}, bf16[8,3,16,128]{3,2,1,0:T(8,128)(2,1)}, u32[]{:S(2)}, u32[]{:S(2)}) collective-permute-start(bf16[8,3,16,128]{3,2,1,0:T(8,128)(2,1)} %get-tuple-element.406), channel_id=1, source_target_pairs={{4,0},{8,4},{12,8},{5,1},{9,5},{13,9},{6,2},{10,6},{14,10},{7,3},{... | collective-permute-start | bytes 294920 | tf_op jit(solution)/shard_map/ppermute | solution.py:18
  216.9 9.6 %copy-start.9 = (bf16[2048,1,1,64]{0,3,2,1:T(8,128)(2,1)S(1)}, bf16[2048,1,1,64]{0,3,2,1:T(8,128)(2,1)}, u32[]{:S(2)}) copy-start(bf16[2048,1,1,64]{0,3,2,1:T(8,128)(2,1)} %copy.53) | copy-start | bytes 786436
  229.1 5.4 %copy-start.10 = (bf16[384,192]{0,1:T(8,128)(2,1)S(1)}, bf16[384,192]{0,1:T(8,128)(2,1)}, u32[]{:S(2)}) copy-start(bf16[384,192]{0,1:T(8,128)(2,1)} %param.16) | copy-start | bytes 442372
  230.3 182.4 %reduce-scatter.4.cloned.1.call-start = ((), (), s32[]{:S(2)}) async-start(), calls=%async_computation.2 | async-start | bytes 3932160
  279.1 1.4 copy-start.5
Sparse Core Ops, SparseCore 0:
  230.5 102.9 all-reduce.1
Sparse Core Ops, SparseCore 1:
  279.2 42.6 reduce-scatter.3
where the time goes:
time: 432 us; the launch traced here: 430 us
  local copies, waits for them, and re-layouts  141 us (33%)
  blocking collectives  129 us (30%)
  matrix products  57 us (13%)
  other arithmetic  38.5 us (9%)
  starting transfers between devices  35 us (8%)
  between operations  15.9 us (4%)
  waiting for transfers between devices  13.2 us (3%)
    psum x1, blocking collectives, shards(): lax.psum(part_output.astype(jnp.bfloat16), ('gx', 'gy')).astype(jnp.float32)  129 us
    unnamed x34, local copies, waits for them, and re-layouts  60.2 us
    ppermute x6, starting transfers between devices, extended(): lax.ppermute(lax.slice_in_dim(block, block.shape[dim] - width, None, axis...  27.2 us
    dot_general x4, matrix products, attend_block(): jnp.einsum('qhe,khe->hqk', query_block, keys_block, preferred_element_typ...  23.3 us
    another operation x4, local copies, waits for them, and re-layouts, attend_block(): jnp.stack([key_gradient, value_gradient], axis=2)  13.1 us
    reshape x4, local copies, waits for them, and re-layouts, attend_block(): jnp.stack([key_gradient, value_gradient], axis=2)  12.6 us
    dynamic_update_slice x4, other arithmetic, attend_block(): lax.dynamic_update_slice_in_dim(pair_sums, previous + pair_gradient, firs...  10.7 us
    ppermute x6, waiting for transfers between devices, extended(): lax.ppermute(lax.slice_in_dim(block, 0, width, axis=dim), axis, backward)  10.7 us
  transfers between devices with their start and end apart: 14, of which 4 were waited for; matrix products, arithmetic and copies ran while one was open for 17% of the time, Pallas kernels for 0%

commit v1 on v0

--- a/solution.py
+++ b/solution.py
@@ -186,7 +186,9 @@
     )
     summed_input, summed_output = (
         lax.psum(part_input.astype(jnp.bfloat16), ("gx", "gy")).astype(jnp.float32),
-        lax.psum(part_output.astype(jnp.bfloat16), ("gx", "gy")).astype(jnp.float32),
+        jnp.sum(lax.all_gather(part_output.astype(jnp.bfloat16), ("gx", "gy")), axis=0).astype(
+            jnp.float32
+        ),
     )
     normaliser = (token_count * lax.axis_size("gx") * lax.axis_size("gy")) ** (-0.5)
     return (token_gradient, summed_input * normaliser, summed_output * normaliser)

time: 432 us -> 411 us (0.951)
  blocking collectives: 129 us -> 0 us
  waiting for transfers between devices: 13.2 us -> 119 us
    psum x1 -> x0, blocking collectives: 129 us -> none  [shards(): lax.psum(part_output.astype(jnp.bfloat16), ('gx', 'gy')).astype(jnp.float32)]
    all_gather x0 -> x1, waiting for transfers between devices: none -> 55.9 us  [shards(): lax.all_gather(part_output.astype(jnp.bfloat16), ('gx', 'gy'))]
    psum x1, waiting for transfers between devices: 0.01 us -> 49.6 us  [shards(): lax.psum(part_input.astype(jnp.bfloat16), ('gx', 'gy')).astype(jnp.float32)]
  transfers between devices with their start and end apart: 14 -> 15, of which waited for: 4 -> 6; matrix products, arithmetic and copies ran while one was open for 17% -> 19% of each run, Pallas kernels for 0% -> 0%
where the time goes in v1:
time: 411 us; the launch traced here: 408 us
  local copies, waits for them, and re-layouts  140 us (34%)
  waiting for transfers between devices  119 us (29%)
  matrix products  58 us (14%)
  other arithmetic  40.1 us (10%)
  starting transfers between devices  35 us (9%)
  between operations  15.9 us (4%)
    unnamed x34, local copies, waits for them, and re-layouts  58.8 us
    all_gather x1, waiting for transfers between devices, shards(): lax.all_gather(part_output.astype(jnp.bfloat16), ('gx', 'gy'))  55.9 us
    psum x1, waiting for transfers between devices, shards(): lax.psum(part_input.astype(jnp.bfloat16), ('gx', 'gy')).astype(jnp.float32)  49.6 us
    ppermute x6, starting transfers between devices, extended(): lax.ppermute(lax.slice_in_dim(block, block.shape[dim] - width, None, axis...  27.2 us
    dot_general x4, matrix products, attend_block(): jnp.einsum('qhe,khe->hqk', query_block, keys_block, preferred_element_typ...  23.3 us
    another operation x4, local copies, waits for them, and re-layouts, attend_block(): jnp.stack([key_gradient, value_gradient], axis=2)  13.1 us
    reshape x4, local copies, waits for them, and re-layouts, attend_block(): jnp.stack([key_gradient, value_gradient], axis=2)  12.6 us
    dynamic_update_slice x4, other arithmetic, attend_block(): lax.dynamic_update_slice_in_dim(pair_sums, previous + pair_gradient, firs...  10.7 us
  transfers between devices with their start and end apart: 15, of which 6 were waited for; matrix products, arithmetic and copies ran while one was open for 19% of the time, Pallas kernels for 0%

profile of v1, /device:TPU:0, one launch (start us, length us, event | category | flops | bytes accessed | tf_op | source)
XLA Modules:
  0.0 407.8 jit_solution(9555364672215945327)
XLA Ops:
  8.9 1.5 fusion.17
  11.0 3.5 collective-permute-start.4
  15.8 1.7 convolution_convert_fusion
  24.8 5.9 %collective-permute-start = (bf16[3,16,16,128]{3,2,1,0:T(8,128)(2,1)}, bf16[3,16,16,128]{3,2,1,0:T(8,128)(2,1)}, u32[]{:S(2)}, u32[]{:S(2)}) collective-permute-start(bf16[3,16,16,128]{3,2,1,0:T(8,128)(2,1)} %slice.209), channel_id=1, source_target_pairs={{0,16},{16,32},{32,48},{48,64},{64,80},{80,96},{96,112},{1,17},{17... | collective-permute-start | bytes 589832 | tf_op jit(solution)/shard_map/ppermute | solution.py:15
  31.3 1.4 convolution_convert_fusion.1
  41.4 6.2 %collective-permute-start.2 = (bf16[14,3,16,128]{3,2,1,0:T(8,128)(2,1)S(1)}, bf16[14,3,16,128]{3,2,1,0:T(8,128)(2,1)S(1)}, u32[]{:S(2)}, u32[]{:S(2)}) collective-permute-start(bf16[14,3,16,128]{3,2,1,0:T(8,128)(2,1)S(1)} %get-tuple-element.401), channel_id=1, source_target_pairs={{0,4},{4,8},{8,12},{1,5},{5,9},{9,13},{2,6},{6,10},{10,14},{3,7},{... | collective-permute-start | bytes 516104 | tf_op jit(solution)/shard_map/ppermute | solution.py:15
  52.0 1.4 pad_maximum_fusion.8
  53.7 1.4 pad_maximum_fusion.1
  55.2 2.1 reshape.485
  59.0 1.7 broadcast_in_dim.27
  60.7 128.2 %while.23 = (s32[]{:T(128)}, bf16[8,16,16,64]{3,2,1,0:T(8,128)(2,1)}, f32[14,22,16,128]{3,2,1,0:T(8,128)}, bf16[8,16,16,64]{3,2,1,0:T(8,128)(2,1)}, bf16[14,22,1...) while((s32[]{:T(128)}, ...), condition=%wide.region_4.5_spmd.clone.clone, body=%wide.region_0.4_spmd.clone.clone.sunk | while | flops 1152845056 | bytes 82846784 | solution.py:152
  63.6 2.5 constant_dynamic-slice_fusion.8
  66.3 5.8 %fusion.85 = (f32[512]{0:T(512)S(1)}, f32[512,2816]{1,0:T(8,128)S(1)}) fusion(bf16[512,64]{1,0:T(8,128)(2,1)S(1)} %bitcast.151, bf16[2816,1,2,64]{3,0,2,1:T(8,128)(2,1)S(1)} %bitcast.144, pred[2816]{0:T(1024)(128)(4,1)S(1)} %gt.22, s32[2816]{0:T(1024)S(1)} %get-tuple-element.564, s32[512]{0:T(512)S(1)} %get-tuple-element.565, ...), kind=kOutput, calls=%fused_computation.123.clone.1 | convolution fusion | flops 214826496 | bytes 6667264 | tf_op jit(solution)/shard_map/while/body/eval_jaxpr/qhe,khe->hqk/dot_general | solution.py:100
  73.1 1.5 divide_convert_fusion.2
  74.5 1.5 copy-done.1
  77.3 2.6 convolution_bitcast_fusion.9
  83.6 3.3 copy.74
  86.9 3.2 reshape.515
  90.1 2.7 add_dynamic-update-slice_fusion.2
  95.7 2.5 constant_dynamic-slice_fusion.8
  98.4 5.8 %fusion.85 = (f32[512]{0:T(512)S(1)}, f32[512,2816]{1,0:T(8,128)S(1)}) fusion(bf16[512,64]{1,0:T(8,128)(2,1)S(1)} %bitcast.151, bf16[2816,1,2,64]{3,0,2,1:T(8,128)(2,1)S(1)} %bitcast.144, pred[2816]{0:T(1024)(128)(4,1)S(1)} %gt.22, s32[2816]{0:T(1024)S(1)} %get-tuple-element.564, s32[512]{0:T(512)S(1)} %get-tuple-element.565, ...), kind=kOutput, calls=%fused_computation.123.clone.1 | convolution fusion | flops 214826496 | bytes 6667264 | tf_op jit(solution)/shard_map/while/body/eval_jaxpr/qhe,khe->hqk/dot_general | solution.py:100
  105.1 1.5 divide_convert_fusion.2
  106.6 1.5 copy-done.1
  109.3 2.6 convolution_bitcast_fusion.9
  115.7 3.3 copy.74
  119.0 3.2 reshape.515
  122.1 2.7 add_dynamic-update-slice_fusion.2
  127.7 2.5 constant_dynamic-slice_fusion.8
  130.4 5.8 %fusion.85 = (f32[512]{0:T(512)S(1)}, f32[512,2816]{1,0:T(8,128)S(1)}) fusion(bf16[512,64]{1,0:T(8,128)(2,1)S(1)} %bitcast.151, bf16[2816,1,2,64]{3,0,2,1:T(8,128)(2,1)S(1)} %bitcast.144, pred[2816]{0:T(1024)(128)(4,1)S(1)} %gt.22, s32[2816]{0:T(1024)S(1)} %get-tuple-element.564, s32[512]{0:T(512)S(1)} %get-tuple-element.565, ...), kind=kOutput, calls=%fused_computation.123.clone.1 | convolution fusion | flops 214826496 | bytes 6667264 | tf_op jit(solution)/shard_map/while/body/eval_jaxpr/qhe,khe->hqk/dot_general | solution.py:100
  137.2 1.5 divide_convert_fusion.2
  138.7 1.5 copy-done.1
  141.4 2.6 convolution_bitcast_fusion.9
  147.8 3.3 copy.74
  151.0 3.2 reshape.515
  154.2 2.7 add_dynamic-update-slice_fusion.2
  159.8 2.5 constant_dynamic-slice_fusion.8
  162.5 5.8 %fusion.85 = (f32[512]{0:T(512)S(1)}, f32[512,2816]{1,0:T(8,128)S(1)}) fusion(bf16[512,64]{1,0:T(8,128)(2,1)S(1)} %bitcast.151, bf16[2816,1,2,64]{3,0,2,1:T(8,128)(2,1)S(1)} %bitcast.144, pred[2816]{0:T(1024)(128)(4,1)S(1)} %gt.22, s32[2816]{0:T(1024)S(1)} %get-tuple-element.564, s32[512]{0:T(512)S(1)} %get-tuple-element.565, ...), kind=kOutput, calls=%fused_computation.123.clone.1 | convolution fusion | flops 214826496 | bytes 6667264 | tf_op jit(solution)/shard_map/while/body/eval_jaxpr/qhe,khe->hqk/dot_general | solution.py:100
  169.2 1.5 divide_convert_fusion.2
  170.7 1.5 copy-done.1
  173.4 2.6 convolution_bitcast_fusion.9
  179.8 3.3 copy.74
  183.1 3.2 reshape.515
  186.2 2.7 add_dynamic-update-slice_fusion.2
  188.9 2.0 convert.14
  191.0 3.6 collective-permute-start.8
  196.0 2.5 collective-permute-done.8
  198.5 7.3 %collective-permute-done.9 = bf16[3,22,16,128]{3,2,1,0:T(8,128)(2,1)S(1)} collective-permute-done((bf16[3,22,16,128]{3,2,1,0:T(8,128)(2,1)S(1)}, bf16[3,22,16,128]{3,2,1,0:T(8,128)(2,1)S(1)}, u32[]{:S(2)}, u32[]{:S(2)}) %collective-permute-start.9) | collective-permute-done | bytes 270368 | tf_op jit(solution)/shard_map/ppermute | solution.py:18
  206.8 6.8 %collective-permute-start.10 = (bf16[8,3,16,128]{3,2,1,0:T(8,128)(2,1)}, bf16[8,3,16,128]{3,2,1,0:T(8,128)(2,1)}, u32[]{:S(2)}, u32[]{:S(2)}) collective-permute-start(bf16[8,3,16,128]{3,2,1,0:T(8,128)(2,1)} %get-tuple-element.405), channel_id=1, source_target_pairs={{0,4},{4,8},{8,12},{1,5},{5,9},{9,13},{2,6},{6,10},{10,14},{3,7},{... | collective-permute-start | bytes 294920 | tf_op jit(solution)/shard_map/ppermute | solution.py:15
  216.9 3.0 collective-permute-done.11
  219.9 1.6 fusion.13
  221.5 1.7 fusion.12
  223.2 2.5 reshape.489
  227.9 2.4 fusion.9
  230.4 2.5 copy.55
  232.9 4.1 convert_element_type.114
  237.0 2.4 fusion.14
  239.3 20.3 %copy.58 = f32[8,16,16,384]{2,1,0,3:T(8,128)} copy(f32[8,16,16,384]{3,2,1,0:T(8,128)} %fusion.14) | data formatting | bytes 6291456
  259.7 21.8 %reshape.512 = f32[384,2048]{1,0:T(8,128)} reshape(f32[384,8,16,16]{3,2,1,0:T(8,128)} %bitcast.148) | data formatting | bytes 6291456
  281.5 49.6 %all-reduce.2.cloned.1.call-done = bf16[384,192]{0,1:T(8,128)(2,1)} async-done(((bf16[384,192]{0,1:T(8,128)(2,1)}), bf16[384,192]{0,1:T(8,128)(2,1)}) %all-reduce.2.cloned.1.call-update) | async-done | bytes 147472 | tf_op jit(solution)/shard_map/psum | solution.py:188
  331.1 1.6 convert_multiply_fusion
  332.7 55.9 %all-gather.3.cloned.1.call-done = bf16[2048,384]{1,0:T(8,128)(2,1)} async-done(((bf16[64,384]{1,0:T(8,128)(2,1)}), bf16[2048,384]{1,0:T(8,128)(2,1)}) %all-gather.3.cloned.1.call-update) | async-done | bytes 1572880 | tf_op jit(solution)/shard_map/all_gather | solution.py:189
  388.7 1.6 reduce_sum.34
  391.0 4.6 %reshape.513 = bf16[96,8,16,16]{3,2,1,0:T(8,128)(2,1)} reshape(f32[96,2048]{1,0:T(8,128)} %reduce-scatter.4.cloned.1.call-done) | data formatting | bytes 1179648
  395.6 4.8 %copy.59 = bf16[8,16,16,96]{3,2,1,0:T(8,128)(2,1)} copy(bf16[8,16,16,96]{2,1,0,3:T(8,128)(2,1)} %bitcast.155) | data formatting | bytes 786432
  (160 shorter events, 69.9 us)
Async XLA Ops:
  8.0 7.8 %copy-start = (bf16[8,16,16,384]{3,2,1,0:T(8,128)(2,1)S(1)}, bf16[8,16,16,384]{3,2,1,0:T(8,128)(2,1)}, u32[]{:S(2)}) copy-start(bf16[8,16,16,384]{3,2,1,0:T(8,128)(2,1)} %param.15) | copy-start | bytes 4718596
  8.0 323.1 %all-reduce.2.cloned.1.call-start = ((), (), s32[]{:S(2)}) async-start(), calls=%async_computation.1 | async-start | bytes 294912 | tf_op jit(solution)/shard_map/psum | solution.py:188
  10.3 5.4 %copy-start.11 = (bf16[8,16,16]{2,1,0:T(8,128)(2,1)}, bf16[8,16,16]{2,1,0:T(8,128)(2,1)S(1)}, u32[]{:S(2)}) copy-start(bf16[8,16,16]{2,1,0:T(8,128)(2,1)S(1)} %fusion.17) | copy-start | bytes 12292
  11.0 24.1 %collective-permute-start.4 = (bf16[3,16,16]{2,1,0:T(8,128)(2,1)}, bf16[3,16,16]{2,1,0:T(8,128)(2,1)S(1)}, u32[]{:S(2)}, u32[]{:S(2)}) collective-permute-start(bf16[3,16,16]{2,1,0:T(8,128)(2,1)} %get-tuple-element.409), channel_id=1, source_target_pairs={{0,16},{16,32},{32,48},{48,64},{64,80},{80,96},{96,112},{1,17},{17... | collective-permute-start | bytes 4616 | tf_op jit(solution)/shard_map/ppermute | solution.py:15
  14.5 20.6 %collective-permute-start.5 = (bf16[3,16,16]{2,1,0:T(8,128)(2,1)}, bf16[3,16,16]{2,1,0:T(8,128)(2,1)}, u32[]{:S(2)}, u32[]{:S(2)}) collective-permute-start(bf16[3,16,16]{2,1,0:T(8,128)(2,1)} %get-tuple-element.410), channel_id=1, source_target_pairs={{16,0},{32,16},{48,32},{64,48},{80,64},{96,80},{112,96},{17,1},{33... | collective-permute-start | bytes 4616 | tf_op jit(solution)/shard_map/ppermute | solution.py:18
  15.8 15.5 %copy-start.4 = (bf16[8,16,16,384]{3,2,1,0:T(8,128)(2,1)S(1)}, bf16[8,16,16,384]{3,2,1,0:T(8,128)(2,1)}, u32[]{:S(2)}) copy-start(bf16[8,16,16,384]{3,2,1,0:T(8,128)(2,1)} %param.19) | copy-start | bytes 4718596
  17.5 0.9 copy-start.5
  21.4 18.1 %collective-permute-start.1 = (bf16[3,16,16,128]{3,2,1,0:T(8,128)(2,1)}, bf16[3,16,16,128]{3,2,1,0:T(8,128)(2,1)}, u32[]{:S(2)}, u32[]{:S(2)}) collective-permute-start(bf16[3,16,16,128]{3,2,1,0:T(8,128)(2,1)} %slice.212), channel_id=1, source_target_pairs={{16,0},{32,16},{48,32},{64,48},{80,64},{96,80},{112,96},{17,1},{33... | collective-permute-start | bytes 589832 | tf_op jit(solution)/shard_map/ppermute | solution.py:18
  24.8 13.6 %collective-permute-start = (bf16[3,16,16,128]{3,2,1,0:T(8,128)(2,1)}, bf16[3,16,16,128]{3,2,1,0:T(8,128)(2,1)}, u32[]{:S(2)}, u32[]{:S(2)}) collective-permute-start(bf16[3,16,16,128]{3,2,1,0:T(8,128)(2,1)} %slice.209), channel_id=1, source_target_pairs={{0,16},{16,32},{32,48},{48,64},{64,80},{80,96},{96,112},{1,17},{17... | collective-permute-start | bytes 589832 | tf_op jit(solution)/shard_map/ppermute | solution.py:15
  32.7 2.4 copy-start.12
  35.8 16.2 %collective-permute-start.6 = (bf16[14,3,16]{2,1,0:T(4,128)(2,1)S(1)}, bf16[14,3,16]{2,1,0:T(4,128)(2,1)S(1)}, u32[]{:S(2)}, u32[]{:S(2)}) collective-permute-start(bf16[14,3,16]{2,1,0:T(4,128)(2,1)S(1)} %get-tuple-element.407), channel_id=1, source_target_pairs={{0,4},{4,8},{8,12},{1,5},{5,9},{9,13},{2,6},{6,10},{10,14},{3,7},{... | collective-permute-start | bytes 4040 | tf_op jit(solution)/shard_map/ppermute | solution.py:15
  37.1 14.9 %collective-permute-start.7 = (bf16[14,3,16]{2,1,0:T(4,128)(2,1)S(1)}, bf16[14,3,16]{2,1,0:T(4,128)(2,1)S(1)}, u32[]{:S(2)}, u32[]{:S(2)}) collective-permute-start(bf16[14,3,16]{2,1,0:T(4,128)(2,1)S(1)} %get-tuple-element.408), channel_id=1, source_target_pairs={{4,0},{8,4},{12,8},{5,1},{9,5},{13,9},{6,2},{10,6},{14,10},{7,3},{... | collective-permute-start | bytes 4040 | tf_op jit(solution)/shard_map/ppermute | solution.py:18
  40.4 1.0 copy-start.6
  41.4 12.0 %collective-permute-start.2 = (bf16[14,3,16,128]{3,2,1,0:T(8,128)(2,1)S(1)}, bf16[14,3,16,128]{3,2,1,0:T(8,128)(2,1)S(1)}, u32[]{:S(2)}, u32[]{:S(2)}) collective-permute-start(bf16[14,3,16,128]{3,2,1,0:T(8,128)(2,1)S(1)} %get-tuple-element.401), channel_id=1, source_target_pairs={{0,4},{4,8},{8,12},{1,5},{5,9},{9,13},{2,6},{6,10},{10,14},{3,7},{... | collective-permute-start | bytes 516104 | tf_op jit(solution)/shard_map/ppermute | solution.py:15
  47.6 6.2 %collective-permute-start.3 = (bf16[14,3,16,128]{3,2,1,0:T(8,128)(2,1)S(1)}, bf16[14,3,16,128]{3,2,1,0:T(8,128)(2,1)}, u32[]{:S(2)}, u32[]{:S(2)}) collective-permute-start(bf16[14,3,16,128]{3,2,1,0:T(8,128)(2,1)S(1)} %get-tuple-element.402), channel_id=1, source_target_pairs={{4,0},{8,4},{12,8},{5,1},{9,5},{13,9},{6,2},{10,6},{14,10},{7,3},{... | collective-permute-start | bytes 516104 | tf_op jit(solution)/shard_map/ppermute | solution.py:18
  57.2 3.5 copy-start.13
  74.5 1.6 copy-start.1
  77.2 2.7 copy-start.2
  106.6 1.6 copy-start.1
  109.3 2.7 copy-start.2
  138.7 1.6 copy-start.1
  141.4 2.7 copy-start.2
  170.7 1.6 copy-start.1
  173.4 2.7 copy-start.2
  188.9 6.9 %copy-start.3 = (f32[14,22,16,128]{3,2,1,0:T(8,128)S(1)}, f32[14,22,16,128]{3,2,1,0:T(8,128)}, u32[]{:S(2)}) copy-start(f32[14,22,16,128]{3,2,1,0:T(8,128)} %get-tuple-element.223) | copy-start | bytes 7569412
  191.0 7.5 %collective-permute-start.8 = (bf16[3,22,16,128]{3,2,1,0:T(8,128)(2,1)S(1)}, bf16[3,22,16,128]{3,2,1,0:T(8,128)(2,1)S(1)}, u32[]{:S(2)}, u32[]{:S(2)}) collective-permute-start(bf16[3,22,16,128]{3,2,1,0:T(8,128)(2,1)S(1)} %get-tuple-element.399), channel_id=1, source_target_pairs={{0,16},{16,32},{32,48},{48,64},{64,80},{80,96},{96,112},{1,17},{17... | collective-permute-start | bytes 811016 | tf_op jit(solution)/shard_map/ppermute | solution.py:15
  194.5 11.3 %collective-permute-start.9 = (bf16[3,22,16,128]{3,2,1,0:T(8,128)(2,1)S(1)}, bf16[3,22,16,128]{3,2,1,0:T(8,128)(2,1)S(1)}, u32[]{:S(2)}, u32[]{:S(2)}) collective-permute-start(bf16[3,22,16,128]{3,2,1,0:T(8,128)(2,1)S(1)} %get-tuple-element.400), channel_id=1, source_target_pairs={{16,0},{32,16},{48,32},{64,48},{80,64},{96,80},{112,96},{17,1},{33... | collective-permute-start | bytes 811016 | tf_op jit(solution)/shard_map/ppermute | solution.py:18
  205.9 9.0 %copy-start.7 = (bf16[8,16,16,64]{3,2,1,0:T(8,128)(2,1)S(1)}, bf16[8,16,16,64]{3,2,1,0:T(8,128)(2,1)}, u32[]{:S(2)}) copy-start(bf16[8,16,16,64]{3,2,1,0:T(8,128)(2,1)} %get-tuple-element.222) | copy-start | bytes 786436
  206.8 10.1 %collective-permute-start.10 = (bf16[8,3,16,128]{3,2,1,0:T(8,128)(2,1)}, bf16[8,3,16,128]{3,2,1,0:T(8,128)(2,1)}, u32[]{:S(2)}, u32[]{:S(2)}) collective-permute-start(bf16[8,3,16,128]{3,2,1,0:T(8,128)(2,1)} %get-tuple-element.405), channel_id=1, source_target_pairs={{0,4},{4,8},{8,12},{1,5},{5,9},{9,13},{2,6},{6,10},{10,14},{3,7},{... | collective-permute-start | bytes 294920 | tf_op jit(solution)/shard_map/ppermute | solution.py:15
  213.6 6.3 %collective-permute-start.11 = (bf16[8,3,16,128]{3,2,1,0:T(8,128)(2,1)}, bf16[8,3,16,128]{3,2,1,0:T(8,128)(2,1)}, u32[]{:S(2)}, u32[]{:S(2)}) collective-permute-start(bf16[8,3,16,128]{3,2,1,0:T(8,128)(2,1)} %get-tuple-element.406), channel_id=1, source_target_pairs={{4,0},{8,4},{12,8},{5,1},{9,5},{13,9},{6,2},{10,6},{14,10},{7,3},{... | collective-permute-start | bytes 294920 | tf_op jit(solution)/shard_map/ppermute | solution.py:18
  216.9 9.6 %copy-start.9 = (bf16[2048,1,1,64]{0,3,2,1:T(8,128)(2,1)S(1)}, bf16[2048,1,1,64]{0,3,2,1:T(8,128)(2,1)}, u32[]{:S(2)}) copy-start(bf16[2048,1,1,64]{0,3,2,1:T(8,128)(2,1)} %copy.53) | copy-start | bytes 786436
  226.5 1.3 copy-start.8
  227.8 160.9 %all-gather.3.cloned.1.call-start = ((), (), s32[]{:S(2)}) async-start(), calls=%async_computation.2 | async-start | bytes 1622016 | tf_op jit(solution)/shard_map/all_gather | solution.py:189
  230.3 6.7 %copy-start.10 = (bf16[384,192]{0,1:T(8,128)(2,1)S(1)}, bf16[384,192]{0,1:T(8,128)(2,1)}, u32[]{:S(2)}) copy-start(bf16[384,192]{0,1:T(8,128)(2,1)} %param.16) | copy-start | bytes 442372
  230.3 160.6 %reduce-scatter.4.cloned.1.call-start = ((), (), s32[]{:S(2)}) async-start(), calls=%async_computation.3 | async-start | bytes 3932160
Sparse Core Ops, SparseCore 0:
  227.9 103.1 all-reduce.1
  333.4 55.2 all-gather.2
Sparse Core Ops, SparseCore 1:
  281.6 42.7 reduce-scatter.3
